TPU v7x, 512 devices: a whole 4x4x16 slice. The times are simulated.
512 devices in a mesh: pipe: 8 (over y, core), ctx: 32 (over x, z_lo), tp: 2 (over z_hi).
Axes of the slice: x: 4, y: 4, z: 16 (z_hi: 2, z_lo: 8; z = z_hi * 8 + z_lo), core: 2. Of those that a mesh axis runs over, the one named last changes fastest.
Arguments:
- stream: bfloat16 [8, 4096, 4096], P('pipe', 'ctx', 'tp'), may hold values from -6 to 6
- queries: bfloat16 [8, 4096, 4096], P('pipe', 'ctx', 'tp'), may hold values from -5 to 5
- keys: bfloat16 [8, 4096, 1024], P('pipe', 'ctx', 'tp'), may hold values from -5 to 5
- values: bfloat16 [8, 4096, 1024], P('pipe', 'ctx', 'tp'), may hold values from -6 to 6
- segments: int32 [8, 4096], P('pipe', 'ctx'), may hold values from 0 to 5, never falling along the last dimension, each value on 1 to 2048 neighbouring positions
- norm_gain: bfloat16 [4096], P('tp'), may hold values from 0.25 to 1.75
Outputs:
- arrived: bfloat16 [8, 4096, 4096], P('pipe', 'ctx', 'tp')
- normed: bfloat16 [8, 4096, 4096], P('pipe', 'ctx', 'tp')
Inputs may be any that keep to these rules, and one draw needn't show every extreme that they name: `segments`: in each section's micro-batch the document number never falls along positions; each document holds 1 to half of 4096 positions, and one holds exactly half of 4096.
All inputs are finite; a program needn't handle non-finite values.
Results may differ from a plain program's by a relative error of at most 0.006.
Values may be sent and summed in bfloat16 or wider, within the bound.
A program may use at most 128 MiB of HBM per device.

v0:
```python
import jax
import jax.numpy as jnp
from jax import lax
from jax.sharding import PartitionSpec as P

QUERY_HEADS = 32
HEAD_SIZE = 128


def from_behind(block, axis, distance):
    devices = range(lax.axis_size(axis))
    route = [((i - distance) % len(devices), i) for i in devices]
    return lax.ppermute(block, axis, route)


def per_device(stream, queries, keys, values, segments, norm_gain):
    row_count = stream.shape[1]
    kv_width = keys.shape[2]
    kv_heads = kv_width // HEAD_SIZE
    query_group_size = queries.shape[2] // kv_width
    score_scale = HEAD_SIZE ** (-0.5)
    ctx_index = lax.axis_index("ctx")
    query_head_stack = (
        queries[0]
        .reshape(row_count, kv_heads, query_group_size, HEAD_SIZE)
        .transpose(1, 2, 0, 3)
        .reshape(kv_heads, query_group_size * row_count, HEAD_SIZE)
    )
    own_pos = ctx_index * row_count + jnp.arange(row_count, dtype=jnp.int32)
    query_pos = jnp.tile(own_pos, query_group_size)
    query_seg = jnp.tile(segments[0], query_group_size)
    query_row_block = query_group_size * row_count
    key_piece = lax.all_gather(keys[0], "ctx", axis=0, tiled=True)
    running_max = jnp.full((kv_heads, query_row_block), -1e30, jnp.float32)
    key_count = key_piece.shape[0]
    key_head_stack = key_piece.reshape(key_count, kv_heads, HEAD_SIZE)
    value_head_stack = lax.all_gather(values[0], "ctx", axis=0, tiled=True).reshape(
        key_count, kv_heads, HEAD_SIZE
    )
    scores = (
        jnp.einsum(
            "hrd,khd->hrk", query_head_stack, key_head_stack, preferred_element_type=jnp.float32
        )
        * score_scale
    )
    key_pos = jnp.arange(key_count, dtype=jnp.int32)
    allowed = (
        (key_pos[None, :] <= query_pos[:, None])
        & (lax.all_gather(segments[0], "ctx", axis=0, tiled=True)[None, :] == query_seg[:, None])
        & jnp.bool_(True)
    )
    scores = jnp.where(allowed[None], scores, -1e30)
    new_max = jnp.maximum(running_max, jnp.max(scores, axis=-1))
    weights = jnp.where(allowed[None], jnp.exp(scores - new_max[..., None]), 0.0)
    new_sum = jnp.sum(weights, axis=-1)
    new_acc = jnp.einsum(
        "hrk,khd->hrd",
        weights.astype(jnp.bfloat16),
        value_head_stack,
        preferred_element_type=jnp.float32,
    )
    final_state = (new_max, new_sum, new_acc)
    running_max, running_sum, running_acc = final_state
    mixed = (running_acc / running_sum[..., None]).astype(jnp.bfloat16)
    attended = (
        mixed.reshape(kv_heads, query_group_size, row_count, HEAD_SIZE)
        .transpose(2, 0, 1, 3)
        .reshape(row_count, kv_width * query_group_size)
    )
    attended = lax.optimization_barrier(attended).astype(jnp.float32)
    advanced = (stream[0].astype(jnp.float32) + attended).astype(jnp.bfloat16)
    arrived = from_behind(advanced[None], "pipe", 1)
    wide = arrived.astype(jnp.float32)
    squares = jnp.sum(wide * wide, axis=-1)
    totals = lax.psum(squares, "tp")
    inverse = lax.rsqrt(totals / (QUERY_HEADS * HEAD_SIZE) + 1e-05)
    normed = (wide * inverse[..., None] * norm_gain.astype(jnp.float32)).astype(jnp.bfloat16)
    return (arrived, normed)


def solution(mesh):
    in_specs = (
        P("pipe", "ctx", "tp"),
        P("pipe", "ctx", "tp"),
        P("pipe", "ctx", "tp"),
        P("pipe", "ctx", "tp"),
        P("pipe", "ctx"),
        P("tp"),
    )
    out_specs = (P("pipe", "ctx", "tp"), P("pipe", "ctx", "tp"))
    return jax.shard_map(
        per_device, mesh=mesh, in_specs=in_specs, out_specs=out_specs, check_vma=False
    )
```

profile of v0, /device:TPU:24, one launch (start us, length us, event | category | flops | bytes accessed | tf_op | source)
XLA Modules:
  0.0 487.4 jit_solution(13736906237650311648)
XLA Ops:
  7.2 0.0 all-gather.6.cloned.1.call-start
  7.2 1.7 copy.11
  8.9 0.0 all-gather.8.cloned.1.call-start
  8.9 1.7 copy.13
  10.6 0.0 all-gather.8.cloned.1.call-update
  10.6 1.4 reshape_squeeze.3
  12.0 0.1 copy.10
  12.2 125.3 %all-gather = s32[1,4096]{1,0:T(1,128)S(1)} all-gather(s32[1,128]{1,0:T(1,128)} %param.10), channel_id=2, replica_groups=mesh['pipe'=8,'ctx'=32,'tp'=2] {'ctx'}, dimensions={1}, use_global_device_ids=true | all-gather | bytes 16896 | tf_op jit(solution)/shard_map/all_gather | solution.py:49
  137.5 0.7 broadcast_bitcast_fusion
  138.1 2.2 fusion.6
  140.3 86.9 %all-gather.6.cloned.1.call-done = bf16[1,4096,512]{1,2,0:T(8,128)(2,1)} async-done(((bf16[1,128,512]{1,2,0:T(8,128)(2,1)}), bf16[1,4096,512]{1,2,0:T(8,128)(2,1)}) %all-gather.6.cloned.1.call-update) | async-done | bytes 4194320 | tf_op jit(solution)/shard_map/all_gather | solution.py:33
  227.3 16.7 %fusion = (f32[4,512]{1,0:T(4,128)S(1)}, f32[4,512,4096]{2,1,0:T(8,128)}) fusion(pred[512,4096]{1,0:T(8,128)(4,1)S(1)} %fusion.6, bf16[4,512,128]{2,1,0:T(8,128)(2,1)S(1)} %bitcast.25, bf16[4096,4,128]{0,2,1:T(8,128)(2,1)} %bitcast.24), kind=kOutput, calls=%fused_computation.2 | convolution fusion | flops 2172647424 | bytes 40378368 | tf_op jit(solution)/shard_map/hrd,khd->hrk/dot_general | solution.py:41
  244.0 15.6 %fusion.1 = f32[4,512]{1,0:T(4,128)S(1)} fusion(f32[4,512,4096]{2,1,0:T(8,128)} %get-tuple-element.3, f32[4,512]{1,0:T(4,128)S(1)} %broadcast_maximum_fusion, pred[512,4096]{1,0:T(8,128)(4,1)S(1)} %fusion.6), kind=kLoop, calls=%fused_computation.3 | loop fusion | flops 41940992 | bytes 35667968 | tf_op jit(solution)/shard_map/reduce_sum | solution.py:55
  259.6 179.7 %all-gather.8.cloned.1.call-done = bf16[1,4096,512]{1,2,0:T(8,128)(2,1)} async-done(((bf16[1,128,512]{1,2,0:T(8,128)(2,1)}), bf16[1,4096,512]{1,2,0:T(8,128)(2,1)}) %all-gather.8.cloned.1.call-update) | async-done | bytes 4194320 | tf_op jit(solution)/shard_map/all_gather | solution.py:37
  439.3 16.1 %divide_convert_fusion = bf16[4,512,128]{2,1,0:T(8,128)(2,1)S(1)} fusion(bf16[4096,4,128]{0,2,1:T(8,128)(2,1)} %bitcast.31, f32[4,512,4096]{2,1,0:T(8,128)} %get-tuple-element.3, f32[4,512]{1,0:T(4,128)S(1)} %broadcast_maximum_fusion, pred[512,4096]{1,0:T(8,128)(4,1)S(1)} %fusion.6, f32[4,512]{1,0:T(4,128)S(1)} %fusion.1), kind=kOutput, calls=%fused_computation.16 | convolution fusion | flops 2189950976 | bytes 40386560 | tf_op jit(solution)/shard_map/hrk,khd->hrd/dot_general | solution.py:56
  455.4 0.4 copy.15
  455.8 0.4 reshape.92
  456.2 0.1 fusion.13
  456.4 0.0 collective-permute-start
  456.4 8.6 %collective-permute-done = bf16[1,128,2048]{2,1,0:T(8,128)(2,1)S(1)} collective-permute-done((bf16[1,128,2048]{2,1,0:T(8,128)(2,1)S(1)}, bf16[1,128,2048]{2,1,0:T(8,128)(2,1)S(1)}, u32[]{:S(2)}, u32[]{:S(2)}) %collective-permute-start) | collective-permute-done | bytes 524320 | tf_op jit(solution)/shard_map/ppermute | solution.py:13
  465.0 0.2 fusion.7
  465.2 13.6 %psum.7 = f32[1,128]{1,0:T(1,128)S(1)} all-reduce(f32[1,128]{1,0:T(1,128)S(1)} %bitcast.30), channel_id=1, replica_groups=mesh['pipe'=8,'ctx'=32,'tp'=2] {'tp'}, use_global_device_ids=true, to_apply=%region_3.4 | all-reduce | flops 128 | bytes 1024 | tf_op jit(solution)/shard_map/psum | solution.py:75
  478.8 1.0 fusion.9
  479.8 0.8 copy.19
  (9 shorter events, 0.0 us)
Async XLA Ops:
  7.2 220.1 %all-gather.6.cloned.1.call-start = ((), (), s32[]{:S(2)}) async-start(), calls=%async_computation | async-start | bytes 4325376 | tf_op jit(solution)/shard_map/all_gather | solution.py:33
  8.9 430.4 %all-gather.8.cloned.1.call-start = ((), (), s32[]{:S(2)}) async-start(), calls=%async_computation.1 | async-start | bytes 4325376 | tf_op jit(solution)/shard_map/all_gather | solution.py:37
  439.3 17.0 %copy-start = (bf16[1,128,2048]{2,1,0:T(8,128)(2,1)S(1)}, bf16[1,128,2048]{2,1,0:T(8,128)(2,1)}, u32[]{:S(2)}) copy-start(bf16[1,128,2048]{2,1,0:T(8,128)(2,1)} %param.6) | copy-start | bytes 1572868
  439.3 17.1 %copy-start.1 = (bf16[2048]{0:T(1024)(128)(2,1)S(1)}, bf16[2048]{0:T(1024)(128)(2,1)}, u32[]{:S(2)}) copy-start(bf16[2048]{0:T(1024)(128)(2,1)} %param.11) | copy-start | bytes 12292
  456.4 8.6 %collective-permute-start = (bf16[1,128,2048]{2,1,0:T(8,128)(2,1)S(1)}, bf16[1,128,2048]{2,1,0:T(8,128)(2,1)S(1)}, u32[]{:S(2)}, u32[]{:S(2)}) collective-permute-start(bf16[1,128,2048]{2,1,0:T(8,128)(2,1)S(1)} %fusion.13), channel_id=1, source_target_pairs={{448,0},{0,64},{64,128},{128,192},{192,256},{256,320},{320,384},{3... | collective-permute-start | bytes 1572872 | tf_op jit(solution)/shard_map/ppermute | solution.py:13
Sparse Core Ops, SparseCore 0:
  10.6 216.6 all-gather.5
  229.9 209.3 all-gather.7
where the time goes:
time: 488 us; the launch traced here: 487 us
  waiting for transfers between devices  275 us (56%)
  blocking collectives  139 us (28%)
  matrix products  32.8 us (7%)
  other arithmetic  19.2 us (4%)
  between operations  14.1 us (3%)
  local copies, waits for them, and re-layouts  7.12 us (1%)
    all_gather x1, waiting for transfers between devices, per_device(): lax.all_gather(values[0], 'ctx', axis=0, tiled=True)  180 us
    all_gather x1, blocking collectives, per_device(): lax.all_gather(segments[0], 'ctx', axis=0, tiled=True)[None, :]  125 us
    all_gather x1, waiting for transfers between devices, per_device(): key_piece = lax.all_gather(keys[0], 'ctx', axis=0, tiled=True)  86.9 us
    dot_general x1, matrix products, per_device(): jnp.einsum('hrd,khd->hrk', query_head_stack, key_head_stack, preferred_el...  16.7 us
    dot_general x1, matrix products, per_device(): jnp.einsum('hrk,khd->hrd', weights.astype(jnp.bfloat16), value_head_stack...  16.1 us
    reduce_sum x1, other arithmetic, per_device(): new_sum = jnp.sum(weights, axis=-1)  15.6 us
    psum x1, blocking collectives, per_device(): totals = lax.psum(squares, 'tp')  13.6 us
  transfers between devices with their start and end apart: 3, of which 3 were waited for; matrix products, arithmetic and copies ran while one was open for 8% of the time, Pallas kernels for 0%

commit v1 on v0

v1 whole, which is shorter than its diff:
```python
import functools

import jax
import jax.numpy as jnp
from jax import lax
from jax.experimental import pallas as pl
from jax.experimental.pallas import tpu as pltpu
from jax.sharding import PartitionSpec as P

QUERY_HEADS = 32
HEAD = 128
MESH = pl.DeviceIdType.MESH
NZ = 8
OH_ROWS = 16
FAR = float(2**20)
LOG2E = 1.4426950408889634


def attention_kernel(
    kv_heads,
    group,
    q_ref,
    k_ref,
    v_ref,
    seg_ref,
    stream_ref,
    out_ref,
    qa,
    own,
    buf,
    m_ref,
    acc,
    recv_sem,
    sendz_sem,
    sendx_sem,
):
    rows = q_ref.shape[0]
    ctx = lax.axis_index("ctx")
    n_ctx = lax.axis_size("ctx")
    x = ctx // NZ
    z = ctx % NZ
    right = (ctx + NZ) % n_ctx
    left = (ctx + n_ctx - NZ) % n_ctx

    barrier = pltpu.get_barrier_semaphore()
    for peer in (right, left):
        pl.semaphore_signal(barrier, inc=1, device_id={"ctx": peer}, device_id_type=MESH)

    @pl.when(z < NZ - 1)
    def _():
        pl.semaphore_signal(barrier, inc=1, device_id={"ctx": ctx + 1}, device_id_type=MESH)

    @pl.when(z > 0)
    def _():
        pl.semaphore_signal(barrier, inc=1, device_id={"ctx": ctx - 1}, device_id_type=MESH)

    seg_f = seg_ref[...].astype(jnp.float32)
    doc_rows = lax.broadcasted_iota(jnp.int32, (OH_ROWS, rows), 0).astype(jnp.float32)
    own[0:OH_ROWS, :] = jnp.where(
        doc_rows == jnp.broadcast_to(seg_f, (OH_ROWS, rows)), 1.0, 0.0
    ).astype(jnp.bfloat16)
    for h in range(kv_heads):
        base = OH_ROWS + 2 * HEAD * h
        key_block = k_ref[:, h * HEAD : (h + 1) * HEAD].astype(jnp.float32)
        own[base : base + HEAD, :] = key_block.T.astype(jnp.bfloat16)
        own[base + HEAD : base + 2 * HEAD, :] = v_ref[:, h * HEAD : (h + 1) * HEAD]

    def part(h):
        if h == 0:
            return pl.ds(0, OH_ROWS + 2 * HEAD)
        return pl.ds(OH_ROWS + 2 * HEAD * h, 2 * HEAD)

    def copy_of(src, slot, which, h, sems, sem_row, peer):
        return pltpu.make_async_remote_copy(
            src_ref=src.at[part(h), :],
            dst_ref=buf.at[slot, which, part(h), :],
            send_sem=sems.at[sem_row, h],
            recv_sem=recv_sem.at[slot, which, h],
            device_id={"ctx": peer},
            device_id_type=MESH,
        )

    pl.semaphore_wait(barrier, 2 + jnp.where(z < NZ - 1, 1, 0) + jnp.where(z > 0, 1, 0))

    def up(h):
        return copy_of(own, z, 0, h, sendz_sem, NZ, ctx + 1)

    def across(h):
        return copy_of(own, z, 0, h, sendx_sem, NZ, right)

    for h in range(kv_heads):
        across(h).start()

        @pl.when(z < NZ - 1)
        def _():
            up(h).start()

    seg_col = jnp.broadcast_to(seg_f, (rows, rows)).T
    lane = lax.broadcasted_iota(jnp.int32, (rows, HEAD), 1)
    penalty = jnp.where(
        (lane < OH_ROWS) & (lane.astype(jnp.float32) != seg_col), -FAR, 0.0
    ).astype(jnp.bfloat16)
    for h in range(kv_heads):
        for g in range(group):
            c = (h * group + g) * HEAD
            qa[h, g * rows : (g + 1) * rows, 0:HEAD] = q_ref[:, c : c + HEAD]
            qa[h, g * rows : (g + 1) * rows, HEAD : 2 * HEAD] = penalty

    scale = LOG2E * HEAD ** (-0.5)
    height = group * rows
    ones = jnp.ones((2 * rows, HEAD), jnp.bfloat16)
    pad = jnp.zeros((HEAD - OH_ROWS, 2 * rows), jnp.bfloat16)

    causal = lax.broadcasted_iota(jnp.int32, (height, rows), 0) % rows >= lax.broadcasted_iota(
        jnp.int32, (height, rows), 1
    )
    for h in range(kv_heads):
        base = OH_ROWS + 2 * HEAD * h
        rhs = jnp.concatenate(
            [own[base : base + HEAD, :], own[0:OH_ROWS, :], pad[:, 0:rows]], axis=0
        )
        s = jnp.dot(qa[h], rhs, preferred_element_type=jnp.float32)
        s = jnp.where(causal, s, -FAR)
        top = jnp.broadcast_to(jnp.max(s, axis=1, keepdims=True), (height, HEAD))
        p = jnp.exp2((s - top) * scale).astype(jnp.bfloat16)
        va = jnp.concatenate([own[base + HEAD : base + 2 * HEAD, :], ones[0:rows]], axis=1)
        m_ref[h] = top
        acc[h] = jnp.dot(p, va, preferred_element_type=jnp.float32)

    nowhere = jnp.where(
        lax.broadcasted_iota(jnp.int32, (OH_ROWS, rows), 0) == OH_ROWS - 1, 1.0, 0.0
    ).astype(jnp.bfloat16)

    def slot_of(r, k):
        return (1 - k) * (z - r) + k * (z + r - 1)

    def exists(r, k):
        return r <= (1 - k) * z + k * (NZ - z)

    def forward_z(slot, k, h):
        return copy_of(buf.at[slot, 0], slot, 0, h, sendz_sem, slot, ctx + 1 - 2 * k)

    def forward_x(slot, h):
        return copy_of(buf.at[slot, 0], slot, 1, h, sendx_sem, slot, right)

    def has_next(k):
        return (1 - k) * (NZ - 1 - z) + k * z > 0

    def relay(r):
        def one(k, carry):
            @pl.when(exists(r, k))
            def _():
                slot = slot_of(r, k)
                for h in range(kv_heads):
                    copy_of(buf.at[slot, 0], slot, 0, h, sendz_sem, slot, right).wait_recv()

                    @pl.when(has_next(k))
                    def _():
                        forward_z(slot, k, h).start()

                    forward_x(slot, h).start()

            return carry

        lax.fori_loop(0, 2, one, 0)

    def attend(r):
        def one(k, carry):
            @pl.when(exists(r, k))
            def _():
                slot = slot_of(r, k)
                for h in range(kv_heads):
                    forward_x(slot, h).wait_recv()
                known0 = x >= k
                known1 = x >= k + 1
                oh0 = jnp.where(known0, buf[slot, 0, 0:OH_ROWS, :], nowhere)
                oh1 = jnp.where(known1, buf[slot, 1, 0:OH_ROWS, :], nowhere)
                oh = jnp.concatenate([oh0, oh1], axis=1)
                for h in range(kv_heads):
                    base = OH_ROWS + 2 * HEAD * h
                    kt = jnp.concatenate(
                        [buf[slot, 0, base : base + HEAD, :], buf[slot, 1, base : base + HEAD, :]],
                        axis=1,
                    )
                    rhs = jnp.concatenate([kt, oh, pad], axis=0)
                    s = jnp.dot(qa[h], rhs, preferred_element_type=jnp.float32)
                    old = m_ref[h]
                    top = jnp.maximum(old, jnp.max(s, axis=1, keepdims=True))
                    p = jnp.exp2((s - jnp.concatenate([top, top], axis=1)) * scale)
                    fade = jnp.exp2((old - top) * scale)
                    vals = jnp.concatenate(
                        [
                            buf[slot, 0, base + HEAD : base + 2 * HEAD, :],
                            buf[slot, 1, base + HEAD : base + 2 * HEAD, :],
                        ],
                        axis=0,
                    )
                    va = jnp.concatenate([vals, ones], axis=1)
                    m_ref[h] = top
                    acc[h] = acc[h] * jnp.concatenate([fade, fade], axis=1) + jnp.dot(
                        p.astype(jnp.bfloat16), va, preferred_element_type=jnp.float32
                    )

            return carry

        lax.fori_loop(0, 2, one, 0)

    def step(r, carry):
        relay(r)

        @pl.when(r > 1)
        def _():
            attend(r - 1)

        return carry

    lax.fori_loop(1, NZ + 1, step, 0)
    attend(NZ)

    for h in range(kv_heads):
        for g in range(group):
            c = (h * group + g) * HEAD
            top_rows = slice(g * rows, (g + 1) * rows)
            mixed = acc[h, top_rows, 0:HEAD] / acc[h, top_rows, HEAD : 2 * HEAD]
            mixed = mixed.astype(jnp.bfloat16).astype(jnp.float32)
            out_ref[:, c : c + HEAD] = (
                stream_ref[:, c : c + HEAD].astype(jnp.float32) + mixed
            ).astype(jnp.bfloat16)

    for h in range(kv_heads):
        across(h).wait_send()

        @pl.when(z < NZ - 1)
        def _():
            up(h).wait_send()

    def drain(r, carry):
        def one(k, inner):
            @pl.when(exists(r, k))
            def _():
                slot = slot_of(r, k)
                for h in range(kv_heads):
                    forward_x(slot, h).wait_send()

                    @pl.when(has_next(k))
                    def _():
                        forward_z(slot, k, h).wait_send()

            return inner

        lax.fori_loop(0, 2, one, 0)
        return carry

    lax.fori_loop(1, NZ + 1, drain, 0)


def attend_and_add(stream, queries, keys, values, segments):
    rows = queries.shape[0]
    kv_heads = keys.shape[1] // HEAD
    group = queries.shape[1] // keys.shape[1]
    block_rows = OH_ROWS + 2 * HEAD * kv_heads
    vmem = pl.BlockSpec(memory_space=pltpu.VMEM)
    return pl.pallas_call(
        functools.partial(attention_kernel, kv_heads, group),
        out_shape=jax.ShapeDtypeStruct(stream.shape, jnp.bfloat16),
        in_specs=[vmem] * 5,
        out_specs=vmem,
        scratch_shapes=[
            pltpu.VMEM((kv_heads, group * rows, 2 * HEAD), jnp.bfloat16),
            pltpu.VMEM((block_rows, rows), jnp.bfloat16),
            pltpu.VMEM((NZ, 2, block_rows, rows), jnp.bfloat16),
            pltpu.VMEM((kv_heads, group * rows, HEAD), jnp.float32),
            pltpu.VMEM((kv_heads, group * rows, 2 * HEAD), jnp.float32),
            pltpu.SemaphoreType.DMA((NZ, 2, kv_heads)),
            pltpu.SemaphoreType.DMA((NZ + 1, kv_heads)),
            pltpu.SemaphoreType.DMA((NZ + 1, kv_heads)),
        ],
        compiler_params=pltpu.CompilerParams(
            collective_id=0, has_side_effects=True, vmem_limit_bytes=48 * 1024 * 1024
        ),
    )(queries, keys, values, segments, stream)


def per_device(stream, queries, keys, values, segments, norm_gain):
    advanced = attend_and_add(stream[0], queries[0], keys[0], values[0], segments)
    n_pipe = lax.axis_size("pipe")
    arrived = lax.ppermute(
        advanced[None], "pipe", [((i - 1) % n_pipe, i) for i in range(n_pipe)]
    )
    wide = arrived.astype(jnp.float32)
    squares = jnp.sum(wide * wide, axis=-1)
    totals = lax.psum(squares, "tp")
    inverse = lax.rsqrt(totals / (QUERY_HEADS * HEAD) + 1e-05)
    normed = (wide * inverse[..., None] * norm_gain.astype(jnp.float32)).astype(jnp.bfloat16)
    return (arrived, normed)


def solution(mesh):
    in_specs = (
        P("pipe", "ctx", "tp"),
        P("pipe", "ctx", "tp"),
        P("pipe", "ctx", "tp"),
        P("pipe", "ctx", "tp"),
        P("pipe", "ctx"),
        P("tp"),
    )
    out_specs = (P("pipe", "ctx", "tp"), P("pipe", "ctx", "tp"))
    return jax.shard_map(
        per_device, mesh=mesh, in_specs=in_specs, out_specs=out_specs, check_vma=False
    )
```

time: 488 us -> 100 us (0.20)
  waiting for transfers between devices: 275 us -> 8.57 us
  blocking collectives: 139 us -> 13.6 us
  Pallas kernels: 0 us -> 69.8 us
  matrix products: 32.8 us -> 0 us
  other arithmetic: 19.2 us -> 1.19 us
  between operations: 14.1 us -> 0.68 us
    all_gather x2 -> x0, waiting for transfers between devices: 267 us -> none  [the longest x1 180 us: per_device(): lax.all_gather(values[0], 'ctx', axis=0, tiled=True)]
    all_gather x1 -> x0, blocking collectives: 125 us -> none  [per_device(): lax.all_gather(segments[0], 'ctx', axis=0, tiled=True)[None, :]]
    pallas_call x0 -> x1, Pallas kernels: none -> 69.8 us  [attend_and_add(): pl.pallas_call(functools.partial(attention_kernel, kv_heads, group), out_...]
    dot_general x2 -> x0, matrix products: 32.8 us -> none  [the longest x1 16.7 us: per_device(): jnp.einsum('hrd,khd->hrk', query_head_stack, key_head_stack, preferred_el...]
    reduce_sum x1 -> x0, other arithmetic: 15.6 us -> none  [per_device(): new_sum = jnp.sum(weights, axis=-1)]
  transfers between devices with their start and end apart: 3 -> 1, of which waited for: 3 -> 1; matrix products, arithmetic and copies ran while one was open for 8% -> 0% of each run, Pallas kernels for 0% -> 0%
where the time goes in v1:
time: 100 us; the launch traced here: 99.3 us
  Pallas kernels  69.8 us (70%)
  blocking collectives  13.6 us (14%)
  waiting for transfers between devices  8.57 us (9%)
  local copies, waits for them, and re-layouts  5.33 us (5%)
  other arithmetic  1.19 us (1%)
    pallas_call x1, Pallas kernels, attend_and_add(): pl.pallas_call(functools.partial(attention_kernel, kv_heads, group), out_...  69.8 us
    psum x1, blocking collectives, per_device(): totals = lax.psum(squares, 'tp')  13.6 us
    ppermute x1, waiting for transfers between devices, per_device(): lax.ppermute(advanced[None], 'pipe', [((i - 1) % n_pipe, i) for i in rang...  8.57 us
    unnamed x13, local copies, waits for them, and re-layouts  5.33 us
  transfers between devices with their start and end apart: 1, of which 1 were waited for; matrix products, arithmetic and copies ran while one was open for 0% of the time, Pallas kernels for 0%

profile of v1, /device:TPU:24, one launch (start us, length us, event | category | flops | bytes accessed | tf_op | source)
XLA Modules:
  0.0 99.3 jit_solution(5005787342684238298)
XLA Ops:
  0.6 0.0 copy-start.4
  0.6 0.6 copy-done.4
  1.3 0.0 copy-start
  1.3 1.0 %copy-done = bf16[1,128,2048]{2,1,0:T(8,128)(2,1)S(1)} copy-done((bf16[1,128,2048]{2,1,0:T(8,128)(2,1)S(1)}, bf16[1,128,2048]{2,1,0:T(8,128)(2,1)}, u32[]{:S(2)}) %copy-start) | copy-done | bytes 524312
  2.3 0.0 copy-start.1
  2.3 1.0 %copy-done.1 = bf16[1,128,2048]{2,1,0:T(8,128)(2,1)S(1)} copy-done((bf16[1,128,2048]{2,1,0:T(8,128)(2,1)S(1)}, bf16[1,128,2048]{2,1,0:T(8,128)(2,1)}, u32[]{:S(2)}) %copy-start.1) | copy-done | bytes 524312
  3.4 0.0 copy-start.2
  3.4 0.9 copy-done.2
  4.3 0.0 copy-start.3
  4.3 0.9 copy-done.3
  5.2 0.0 copy-start.5
  5.2 69.8 %shard_map.77 = bf16[128,2048]{1,0:T(8,128)(2,1)S(1)} custom-call(bf16[128,2048]{1,0:T(8,128)(2,1)S(1)} %bitcast.8, bf16[128,512]{1,0:T(8,128)(2,1)S(1)} %bitcast.11, bf16[128,512]{1,0:T(8,128)(2,1)S(1)} %bitcast.12, s32[1,128]{1,0:T(1,128)S(1)} %copy-done.4, bf16[128,2048]{1,0:T(8,128)(2,1)S(1)} %bitcast.9), custom_call_target="tpu_custom_call" | custom-call | tf_op jit(solution)/shard_map/pallas_call | solution.py:263
  75.0 0.0 collective-permute-start
  75.1 0.0 copy-done.5
  75.1 8.6 %collective-permute-done = bf16[1,128,2048]{2,1,0:T(8,128)(2,1)S(1)} collective-permute-done((bf16[1,128,2048]{2,1,0:T(8,128)(2,1)S(1)}, bf16[1,128,2048]{2,1,0:T(8,128)(2,1)S(1)}, u32[]{:S(2)}, u32[]{:S(2)}) %collective-permute-start) | collective-permute-done | bytes 524320 | tf_op jit(solution)/shard_map/ppermute | solution.py:287
  83.7 0.2 fusion
  83.8 13.6 %psum.7 = f32[1,128]{1,0:T(1,128)S(1)} all-reduce(f32[1,128]{1,0:T(1,128)S(1)} %bitcast.13), channel_id=1, replica_groups=mesh['pipe'=8,'ctx'=32,'tp'=2] {'tp'}, use_global_device_ids=true, to_apply=%region_1.0 | all-reduce | flops 128 | bytes 1024 | tf_op jit(solution)/shard_map/psum | solution.py:292
  97.5 1.0 fusion.2
  98.5 0.8 copy.9
  (2 shorter events, 0.0 us)
Async XLA Ops:
  0.6 0.7 copy-start.4
  1.3 1.0 %copy-start = (bf16[1,128,2048]{2,1,0:T(8,128)(2,1)S(1)}, bf16[1,128,2048]{2,1,0:T(8,128)(2,1)}, u32[]{:S(2)}) copy-start(bf16[1,128,2048]{2,1,0:T(8,128)(2,1)} %param.7) | copy-start | bytes 1572868
  2.3 1.0 %copy-start.1 = (bf16[1,128,2048]{2,1,0:T(8,128)(2,1)S(1)}, bf16[1,128,2048]{2,1,0:T(8,128)(2,1)}, u32[]{:S(2)}) copy-start(bf16[1,128,2048]{2,1,0:T(8,128)(2,1)} %param.6) | copy-start | bytes 1572868
  3.4 0.9 copy-start.2
  4.3 0.9 copy-start.3
  5.2 69.9 %copy-start.5 = (bf16[2048]{0:T(1024)(128)(2,1)S(1)}, bf16[2048]{0:T(1024)(128)(2,1)}, u32[]{:S(2)}) copy-start(bf16[2048]{0:T(1024)(128)(2,1)} %param.11) | copy-start | bytes 12292
  75.0 8.6 %collective-permute-start = (bf16[1,128,2048]{2,1,0:T(8,128)(2,1)S(1)}, bf16[1,128,2048]{2,1,0:T(8,128)(2,1)S(1)}, u32[]{:S(2)}, u32[]{:S(2)}) collective-permute-start(bf16[1,128,2048]{2,1,0:T(8,128)(2,1)S(1)} %bitcast.10), channel_id=1, source_target_pairs={{448,0},{0,64},{64,128},{128,192},{192,256},{256,320},{320,384},{3... | collective-permute-start | bytes 1572872 | tf_op jit(solution)/shard_map/ppermute | solution.py:287

commit v2 on v1

--- a/solution.py
+++ b/solution.py
@@ -19,12 +19,21 @@
 def attention_kernel(
     kv_heads,
     group,
+    q_hbm,
+    k_hbm,
+    v_hbm,
+    stream_hbm,
+    seg_ref,
+    gain_ref,
+    arrived_ref,
+    normed_ref,
     q_ref,
     k_ref,
     v_ref,
-    seg_ref,
     stream_ref,
-    out_ref,
+    advanced,
+    square_out,
+    square_in,
     qa,
     own,
     buf,
@@ -33,8 +42,19 @@
     recv_sem,
     sendz_sem,
     sendx_sem,
+    load_sem,
+    pipe_send_sem,
+    pipe_recv_sem,
+    square_send_sem,
+    square_recv_sem,
 ):
     rows = q_ref.shape[0]
+    pipe = lax.axis_index("pipe")
+    n_pipe = lax.axis_size("pipe")
+    tp = lax.axis_index("tp")
+    n_tp = lax.axis_size("tp")
+    following = (pipe + 1) % n_pipe
+    preceding = (pipe + n_pipe - 1) % n_pipe
     ctx = lax.axis_index("ctx")
     n_ctx = lax.axis_size("ctx")
     x = ctx // NZ
@@ -53,6 +73,23 @@
     @pl.when(z > 0)
     def _():
         pl.semaphore_signal(barrier, inc=1, device_id={"ctx": ctx - 1}, device_id_type=MESH)
+
+    for peer in (following, preceding):
+        for half in range(n_tp):
+            pl.semaphore_signal(
+                barrier, inc=1, device_id={"pipe": peer, "tp": half}, device_id_type=MESH
+            )
+
+    loads = [
+        pltpu.make_async_copy(src, dst, load_sem.at[i])
+        for i, (src, dst) in enumerate(
+            ((k_hbm, k_ref), (v_hbm, v_ref), (q_hbm, q_ref), (stream_hbm, stream_ref))
+        )
+    ]
+    for load in loads:
+        load.start()
+    loads[0].wait()
+    loads[1].wait()
 
     seg_f = seg_ref[...].astype(jnp.float32)
     doc_rows = lax.broadcasted_iota(jnp.int32, (OH_ROWS, rows), 0).astype(jnp.float32)
@@ -80,7 +117,7 @@
             device_id_type=MESH,
         )
 
-    pl.semaphore_wait(barrier, 2 + jnp.where(z < NZ - 1, 1, 0) + jnp.where(z > 0, 1, 0))
+    pl.semaphore_wait(barrier, 2 + 2 * n_tp + jnp.where(z < NZ - 1, 1, 0) + jnp.where(z > 0, 1, 0))
 
     def up(h):
         return copy_of(own, z, 0, h, sendz_sem, NZ, ctx + 1)
@@ -95,6 +132,7 @@
         def _():
             up(h).start()
 
+    loads[2].wait()
     seg_col = jnp.broadcast_to(seg_f, (rows, rows)).T
     lane = lax.broadcasted_iota(jnp.int32, (rows, HEAD), 1)
     penalty = jnp.where(
@@ -217,15 +255,47 @@
     lax.fori_loop(1, NZ + 1, step, 0)
     attend(NZ)
 
+    loads[3].wait()
+    width = group * HEAD
+
+    def relay_out(h):
+        columns = pl.ds(h * width, width)
+        return pltpu.make_async_remote_copy(
+            src_ref=advanced.at[:, columns],
+            dst_ref=arrived_ref.at[:, columns],
+            send_sem=pipe_send_sem.at[h],
+            recv_sem=pipe_recv_sem.at[h],
+            device_id={"pipe": following},
+            device_id_type=MESH,
+        )
+
+    squares = jnp.zeros((rows, HEAD), jnp.float32)
     for h in range(kv_heads):
         for g in range(group):
             c = (h * group + g) * HEAD
             top_rows = slice(g * rows, (g + 1) * rows)
             mixed = acc[h, top_rows, 0:HEAD] / acc[h, top_rows, HEAD : 2 * HEAD]
             mixed = mixed.astype(jnp.bfloat16).astype(jnp.float32)
-            out_ref[:, c : c + HEAD] = (
-                stream_ref[:, c : c + HEAD].astype(jnp.float32) + mixed
-            ).astype(jnp.bfloat16)
+            total = (stream_ref[:, c : c + HEAD].astype(jnp.float32) + mixed).astype(jnp.bfloat16)
+            advanced[:, c : c + HEAD] = total
+            wide = total.astype(jnp.float32)
+            squares = squares + wide * wide
+        relay_out(h).start()
+    row_sums = jnp.broadcast_to(jnp.sum(squares, axis=1, keepdims=True), (rows, HEAD))
+    square_out[...] = row_sums.T[0:8, :]
+
+    def sums_out(t):
+        return pltpu.make_async_remote_copy(
+            src_ref=square_out,
+            dst_ref=square_in.at[t],
+            send_sem=square_send_sem.at[t],
+            recv_sem=square_recv_sem.at[t],
+            device_id={"pipe": following, "tp": (tp + t) % n_tp},
+            device_id_type=MESH,
+        )
+
+    for t in range(n_tp):
+        sums_out(n_tp - 1 - t).start()
 
     for h in range(kv_heads):
         across(h).wait_send()
@@ -253,19 +323,49 @@
 
     lax.fori_loop(1, NZ + 1, drain, 0)
 
-
-def attend_and_add(stream, queries, keys, values, segments):
+    for t in range(n_tp):
+        sums_out(t).wait_recv()
+    total = square_in[0, 0:1, :]
+    for t in range(1, n_tp):
+        total = total + square_in[t, 0:1, :]
+    inverse = lax.rsqrt(total / (QUERY_HEADS * HEAD) + 1e-05)
+    inverse = jnp.broadcast_to(inverse, (rows, rows)).T
+    for h in range(kv_heads):
+        relay_out(h).wait_recv()
+        for g in range(group):
+            c = (h * group + g) * HEAD
+            wide = arrived_ref[:, c : c + HEAD].astype(jnp.float32)
+            gain = gain_ref[0:1, c : c + HEAD].astype(jnp.float32)
+            normed_ref[:, c : c + HEAD] = (wide * inverse * gain).astype(jnp.bfloat16)
+    for h in range(kv_heads):
+        relay_out(h).wait_send()
+    for t in range(n_tp):
+        sums_out(t).wait_send()
+
+
+def per_device(stream, queries, keys, values, segments, norm_gain):
+    stream, queries, keys, values = stream[0], queries[0], keys[0], values[0]
     rows = queries.shape[0]
     kv_heads = keys.shape[1] // HEAD
     group = queries.shape[1] // keys.shape[1]
     block_rows = OH_ROWS + 2 * HEAD * kv_heads
+    n_tp = lax.axis_size("tp")
     vmem = pl.BlockSpec(memory_space=pltpu.VMEM)
-    return pl.pallas_call(
+    anywhere = pl.BlockSpec(memory_space=pltpu.HBM)
+    like_stream = jax.ShapeDtypeStruct(stream.shape, jnp.bfloat16)
+    arrived, normed = pl.pallas_call(
         functools.partial(attention_kernel, kv_heads, group),
-        out_shape=jax.ShapeDtypeStruct(stream.shape, jnp.bfloat16),
-        in_specs=[vmem] * 5,
-        out_specs=vmem,
+        out_shape=(like_stream, like_stream),
+        in_specs=[anywhere] * 4 + [vmem] * 2,
+        out_specs=(vmem, vmem),
         scratch_shapes=[
+            pltpu.VMEM(queries.shape, jnp.bfloat16),
+            pltpu.VMEM(keys.shape, jnp.bfloat16),
+            pltpu.VMEM(values.shape, jnp.bfloat16),
+            pltpu.VMEM(stream.shape, jnp.bfloat16),
+            pltpu.VMEM(stream.shape, jnp.bfloat16),
+            pltpu.VMEM((8, rows), jnp.float32),
+            pltpu.VMEM((n_tp, 8, rows), jnp.float32),
             pltpu.VMEM((kv_heads, group * rows, 2 * HEAD), jnp.bfloat16),
             pltpu.VMEM((block_rows, rows), jnp.bfloat16),
             pltpu.VMEM((NZ, 2, block_rows, rows), jnp.bfloat16),
@@ -274,25 +374,17 @@
             pltpu.SemaphoreType.DMA((NZ, 2, kv_heads)),
             pltpu.SemaphoreType.DMA((NZ + 1, kv_heads)),
             pltpu.SemaphoreType.DMA((NZ + 1, kv_heads)),
+            pltpu.SemaphoreType.DMA((4,)),
+            pltpu.SemaphoreType.DMA((kv_heads,)),
+            pltpu.SemaphoreType.DMA((kv_heads,)),
+            pltpu.SemaphoreType.DMA((n_tp,)),
+            pltpu.SemaphoreType.DMA((n_tp,)),
         ],
         compiler_params=pltpu.CompilerParams(
             collective_id=0, has_side_effects=True, vmem_limit_bytes=48 * 1024 * 1024
         ),
-    )(queries, keys, values, segments, stream)
-
-
-def per_device(stream, queries, keys, values, segments, norm_gain):
-    advanced = attend_and_add(stream[0], queries[0], keys[0], values[0], segments)
-    n_pipe = lax.axis_size("pipe")
-    arrived = lax.ppermute(
-        advanced[None], "pipe", [((i - 1) % n_pipe, i) for i in range(n_pipe)]
-    )
-    wide = arrived.astype(jnp.float32)
-    squares = jnp.sum(wide * wide, axis=-1)
-    totals = lax.psum(squares, "tp")
-    inverse = lax.rsqrt(totals / (QUERY_HEADS * HEAD) + 1e-05)
-    normed = (wide * inverse[..., None] * norm_gain.astype(jnp.float32)).astype(jnp.bfloat16)
-    return (arrived, normed)
+    )(queries, keys, values, stream, segments, norm_gain[None])
+    return (arrived[None], normed[None])
 
 
 def solution(mesh):

time: 100 us -> 94.9 us (0.949)
  Pallas kernels: 69.8 us -> 85.8 us
  blocking collectives: 13.6 us -> 0 us
  waiting for transfers between devices: 8.57 us -> 0 us
  local copies, waits for them, and re-layouts: 5.33 us -> 6.81 us
  other arithmetic: 1.19 us -> 0 us
    pallas_call x1, Pallas kernels: 69.8 us -> 85.8 us  [per_device(): pl.pallas_call(functools.partial(attention_kernel, kv_heads, group), out_...]
    psum x1 -> x0, blocking collectives: 13.6 us -> none  [per_device(): totals = lax.psum(squares, 'tp')]
    ppermute x1 -> x0, waiting for transfers between devices: 8.57 us -> none  [per_device(): lax.ppermute(advanced[None], 'pipe', [((i - 1) % n_pipe, i) for i in rang...]
    unnamed x13 -> x14, local copies, waits for them, and re-layouts: 5.33 us -> 6.8 us
  transfers between devices with their start and end apart: 1 -> 0, of which waited for: 1 -> 0; matrix products, arithmetic and copies ran while one was open for 0% -> 0% of each run, Pallas kernels for 0% -> 0%
where the time goes in v2:
time: 94.9 us; the launch traced here: 93.3 us
  Pallas kernels  85.8 us (90%)
  local copies, waits for them, and re-layouts  6.81 us (7%)
    pallas_call x1, Pallas kernels, per_device(): pl.pallas_call(functools.partial(attention_kernel, kv_heads, group), out_...  85.8 us
    unnamed x14, local copies, waits for them, and re-layouts  6.8 us

profile of v2, /device:TPU:24, one launch (start us, length us, event | category | flops | bytes accessed | tf_op | source)
XLA Modules:
  0.0 93.3 jit_solution(16425587347185102706)
XLA Ops:
  0.6 0.0 copy-start.5
  0.6 0.7 copy-done.5
  1.3 0.0 copy-start.4
  1.3 0.6 copy-done.4
  2.0 0.0 copy-start
  2.0 1.0 %copy-done = bf16[1,128,2048]{2,1,0:T(8,128)(2,1)S(1)} copy-done((bf16[1,128,2048]{2,1,0:T(8,128)(2,1)S(1)}, bf16[1,128,2048]{2,1,0:T(8,128)(2,1)}, u32[]{:S(2)}) %copy-start) | copy-done | bytes 524312
  3.0 0.0 copy-start.1
  3.0 1.0 %copy-done.1 = bf16[1,128,2048]{2,1,0:T(8,128)(2,1)S(1)} copy-done((bf16[1,128,2048]{2,1,0:T(8,128)(2,1)S(1)}, bf16[1,128,2048]{2,1,0:T(8,128)(2,1)}, u32[]{:S(2)}) %copy-start.1) | copy-done | bytes 524312
  4.1 0.0 copy-start.2
  4.1 0.9 copy-done.2
  5.0 0.0 copy-start.3
  5.0 0.9 copy-done.3
  5.9 85.8 %shard_map.77 = (bf16[128,2048]{1,0:T(8,128)(2,1)S(1)}, bf16[128,2048]{1,0:T(8,128)(2,1)S(1)}) custom-call(bf16[128,2048]{1,0:T(8,128)(2,1)S(1)} %bitcast.6, bf16[128,512]{1,0:T(8,128)(2,1)S(1)} %bitcast.10, bf16[128,512]{1,0:T(8,128)(2,1)S(1)} %bitcast.11, bf16[128,2048]{1,0:T(8,128)(2,1)S(1)} %bitcast.7, s32[1,128]{1,0:T(1,128)S(1)} %copy-done.4, ...), custom_call_target="tpu_custom_call" | custom-call | tf_op jit(solution)/shard_map/pallas_call | solution.py:356
  91.7 0.8 copy.10
  92.5 0.8 copy.11
  (1 shorter events, 0.0 us)
Async XLA Ops:
  0.6 0.7 copy-start.5
  1.3 0.7 copy-start.4
  2.0 1.0 %copy-start = (bf16[1,128,2048]{2,1,0:T(8,128)(2,1)S(1)}, bf16[1,128,2048]{2,1,0:T(8,128)(2,1)}, u32[]{:S(2)}) copy-start(bf16[1,128,2048]{2,1,0:T(8,128)(2,1)} %param.7) | copy-start | bytes 1572868
  3.0 1.0 %copy-start.1 = (bf16[1,128,2048]{2,1,0:T(8,128)(2,1)S(1)}, bf16[1,128,2048]{2,1,0:T(8,128)(2,1)}, u32[]{:S(2)}) copy-start(bf16[1,128,2048]{2,1,0:T(8,128)(2,1)} %param.6) | copy-start | bytes 1572868
  4.1 0.9 copy-start.2
  5.0 0.9 copy-start.3

commit v3 on v2

v3 whole, which is shorter than its diff:
```python
import functools

import jax
import jax.numpy as jnp
from jax import lax
from jax.experimental import pallas as pl
from jax.experimental.pallas import tpu as pltpu
from jax.sharding import PartitionSpec as P

QUERY_HEADS = 32
HEAD = 128
MESH = pl.DeviceIdType.MESH
NZ = 8
OH_ROWS = 16
FAR = float(2**20)
LOG2E = 1.4426950408889634


def attention_kernel(
    kv_heads,
    group,
    q_hbm,
    k_hbm,
    v_hbm,
    stream_hbm,
    seg_hbm,
    gain_hbm,
    arrived_ref,
    normed_ref,
    q_ref,
    k_ref,
    v_ref,
    stream_ref,
    seg_ref,
    gain_ref,
    advanced,
    square_out,
    square_in,
    qa,
    own,
    passing,
    buf,
    m_ref,
    acc,
    recv_sem,
    sendz_sem,
    sendx_sem,
    pass_recv_sem,
    pass_send_sem,
    load_sem,
    pipe_send_sem,
    pipe_recv_sem,
    square_send_sem,
    square_recv_sem,
):
    rows = q_ref.shape[0]
    pipe = lax.axis_index("pipe")
    n_pipe = lax.axis_size("pipe")
    tp = lax.axis_index("tp")
    n_tp = lax.axis_size("tp")
    following = (pipe + 1) % n_pipe
    preceding = (pipe + n_pipe - 1) % n_pipe
    ctx = lax.axis_index("ctx")
    n_ctx = lax.axis_size("ctx")
    x = ctx // NZ
    z = ctx % NZ
    right = (ctx + NZ) % n_ctx
    left = (ctx + n_ctx - NZ) % n_ctx

    loads = [
        pltpu.make_async_copy(src, dst, load_sem.at[i])
        for i, (src, dst) in enumerate(
            (
                (seg_hbm, seg_ref),
                (k_hbm, k_ref),
                (v_hbm, v_ref),
                (q_hbm, q_ref),
                (stream_hbm, stream_ref),
                (gain_hbm, gain_ref),
            )
        )
    ]
    for load in loads:
        load.start()

    barrier = pltpu.get_barrier_semaphore()
    for peer in (right, left):
        pl.semaphore_signal(barrier, inc=1, device_id={"ctx": peer}, device_id_type=MESH)

    @pl.when(z < NZ - 1)
    def _():
        pl.semaphore_signal(barrier, inc=1, device_id={"ctx": ctx + 1}, device_id_type=MESH)

    @pl.when(z > 0)
    def _():
        pl.semaphore_signal(barrier, inc=1, device_id={"ctx": ctx - 1}, device_id_type=MESH)

    for peer in (following, preceding):
        for half in range(n_tp):
            pl.semaphore_signal(
                barrier, inc=1, device_id={"pipe": peer, "tp": half}, device_id_type=MESH
            )

    def part(h):
        if h == 0:
            return pl.ds(0, OH_ROWS + 2 * HEAD)
        return pl.ds(OH_ROWS + 2 * HEAD * h, 2 * HEAD)

    def send(src, dst, h, send_sem, arrive_sem, peer):
        return pltpu.make_async_remote_copy(
            src_ref=src.at[part(h), :],
            dst_ref=dst.at[part(h), :],
            send_sem=send_sem,
            recv_sem=arrive_sem,
            device_id={"ctx": peer},
            device_id_type=MESH,
        )

    def copy_of(src, slot, which, h, send_sem, peer):
        return send(src, buf.at[slot, which], h, send_sem, recv_sem.at[slot, which, h], peer)

    def up(h):
        return copy_of(own, z, 0, h, sendz_sem.at[NZ, h], ctx + 1)

    def across(h):
        return copy_of(own, z, 0, h, sendx_sem.at[NZ, h], right)

    def pass_first(h):
        return send(own, passing, h, pass_send_sem.at[0, h], pass_recv_sem.at[h], left)

    def pass_second(h):
        return copy_of(passing, z, 1, h, pass_send_sem.at[1, h], left)

    for load in loads[:3]:
        load.wait()
    seg_f = seg_ref[...].astype(jnp.float32)
    doc_rows = lax.broadcasted_iota(jnp.int32, (OH_ROWS, rows), 0).astype(jnp.float32)
    own[0:OH_ROWS, :] = jnp.where(
        doc_rows == jnp.broadcast_to(seg_f, (OH_ROWS, rows)), 1.0, 0.0
    ).astype(jnp.bfloat16)
    for h in range(kv_heads):
        base = OH_ROWS + 2 * HEAD * h
        key_block = k_ref[:, h * HEAD : (h + 1) * HEAD].astype(jnp.float32)
        own[base : base + HEAD, :] = key_block.T.astype(jnp.bfloat16)
        own[base + HEAD : base + 2 * HEAD, :] = v_ref[:, h * HEAD : (h + 1) * HEAD]
        if h == 0:
            pl.semaphore_wait(
                barrier,
                2 + 2 * n_tp + jnp.where(z < NZ - 1, 1, 0) + jnp.where(z > 0, 1, 0),
            )
        across(h).start()

        @pl.when(z < NZ - 1)
        def _():
            up(h).start()

        pass_first(h).start()

    loads[3].wait()
    seg_col = jnp.broadcast_to(seg_f, (rows, rows)).T
    lane = lax.broadcasted_iota(jnp.int32, (rows, HEAD), 1)
    penalty = jnp.where(
        (lane < OH_ROWS) & (lane.astype(jnp.float32) != seg_col), -FAR, 0.0
    ).astype(jnp.bfloat16)
    for h in range(kv_heads):
        for g in range(group):
            c = (h * group + g) * HEAD
            qa[h, g * rows : (g + 1) * rows, 0:HEAD] = q_ref[:, c : c + HEAD]
            qa[h, g * rows : (g + 1) * rows, HEAD : 2 * HEAD] = penalty

    scale = LOG2E * HEAD ** (-0.5)
    height = group * rows
    ones = jnp.ones((2 * rows, HEAD), jnp.bfloat16)
    pad = jnp.zeros((HEAD - OH_ROWS, 2 * rows), jnp.bfloat16)

    causal = lax.broadcasted_iota(jnp.int32, (height, rows), 0) % rows >= lax.broadcasted_iota(
        jnp.int32, (height, rows), 1
    )

    def attend_own(h):
        base = OH_ROWS + 2 * HEAD * h
        rhs = jnp.concatenate(
            [own[base : base + HEAD, :], own[0:OH_ROWS, :], pad[:, 0:rows]], axis=0
        )
        s = jnp.dot(qa[h], rhs, preferred_element_type=jnp.float32)
        s = jnp.where(causal, s, -FAR)
        top = jnp.broadcast_to(jnp.max(s, axis=1, keepdims=True), (height, HEAD))
        p = jnp.exp2((s - top) * scale).astype(jnp.bfloat16)
        va = jnp.concatenate([own[base + HEAD : base + 2 * HEAD, :], ones[0:rows]], axis=1)
        m_ref[h] = top
        acc[h] = jnp.dot(p, va, preferred_element_type=jnp.float32)

    nowhere = jnp.where(
        lax.broadcasted_iota(jnp.int32, (OH_ROWS, rows), 0) == OH_ROWS - 1, 1.0, 0.0
    ).astype(jnp.bfloat16)

    both = jnp.minimum(z, NZ - z)

    def place(t):
        paired = jnp.where(t <= 2 * both, 1, 0)
        r = paired * ((t + 1) // 2) + (1 - paired) * (t - both)
        tall = jnp.where(z > NZ - z, 0, 1)
        k = paired * ((t + 1) % 2) + (1 - paired) * tall
        slot = (1 - k) * (z - r) + k * (z + r - 1)
        onward = (1 - k) * (NZ - 1 - z) + k * z > 0
        first_of_beyond = r + NZ * (1 - k) == 1
        return slot, k, onward, first_of_beyond

    def forward_z(slot, k, h):
        return copy_of(buf.at[slot, 0], slot, 0, h, sendz_sem.at[slot, h], ctx + 1 - 2 * k)

    def forward_x(slot, h):
        return copy_of(buf.at[slot, 0], slot, 1, h, sendx_sem.at[slot, h], right)

    def relay(at, h):
        slot, k, onward, first_of_beyond = at
        across_wait = copy_of(buf.at[slot, 0], slot, 0, h, sendz_sem.at[slot, h], right)
        across_wait.wait_recv()

        @pl.when(onward)
        def _():
            forward_z(slot, k, h).start()

        @pl.when(jnp.logical_not(first_of_beyond))
        def _():
            forward_x(slot, h).start()

    def attend(at, h):
        slot, k, _, _ = at
        forward_x(slot, h).wait_recv()
        oh0 = jnp.where(x >= k, buf[slot, 0, 0:OH_ROWS, :], nowhere)
        oh1 = jnp.where(x >= k + 1, buf[slot, 1, 0:OH_ROWS, :], nowhere)
        oh = jnp.concatenate([oh0, oh1], axis=1)
        base = OH_ROWS + 2 * HEAD * h
        kt = jnp.concatenate(
            [buf[slot, 0, base : base + HEAD, :], buf[slot, 1, base : base + HEAD, :]],
            axis=1,
        )
        rhs = jnp.concatenate([kt, oh, pad], axis=0)
        s = jnp.dot(qa[h], rhs, preferred_element_type=jnp.float32)
        old = m_ref[h]
        top = jnp.maximum(old, jnp.max(s, axis=1, keepdims=True))
        p = jnp.exp2((s - jnp.concatenate([top, top], axis=1)) * scale)
        fade = jnp.exp2((old - top) * scale)
        vals = jnp.concatenate(
            [
                buf[slot, 0, base + HEAD : base + 2 * HEAD, :],
                buf[slot, 1, base + HEAD : base + 2 * HEAD, :],
            ],
            axis=0,
        )
        va = jnp.concatenate([vals, ones], axis=1)
        m_ref[h] = top
        acc[h] = acc[h] * jnp.concatenate([fade, fade], axis=1) + jnp.dot(
            p.astype(jnp.bfloat16), va, preferred_element_type=jnp.float32
        )

    first = place(1)
    for h in range(kv_heads):
        pass_first(h).wait_recv()
        pass_second(h).start()
        relay(first, h)
        attend_own(h)

    def step(t, carry):
        now, before = place(t), place(t - 1)
        for h in range(kv_heads):
            relay(now, h)
            attend(before, h)
        return carry

    lax.fori_loop(2, NZ + 1, step, 0)

    loads[4].wait()
    loads[5].wait()
    width = group * HEAD

    def relay_out(h):
        columns = pl.ds(h * width, width)
        return pltpu.make_async_remote_copy(
            src_ref=advanced.at[:, columns],
            dst_ref=arrived_ref.at[:, columns],
            send_sem=pipe_send_sem.at[h],
            recv_sem=pipe_recv_sem.at[h],
            device_id={"pipe": following},
            device_id_type=MESH,
        )

    last = place(NZ)
    squares = jnp.zeros((rows, HEAD), jnp.float32)
    for h in range(kv_heads):
        attend(last, h)
        for g in range(group):
            c = (h * group + g) * HEAD
            top_rows = slice(g * rows, (g + 1) * rows)
            mixed = acc[h, top_rows, 0:HEAD] / acc[h, top_rows, HEAD : 2 * HEAD]
            mixed = mixed.astype(jnp.bfloat16).astype(jnp.float32)
            total = (stream_ref[:, c : c + HEAD].astype(jnp.float32) + mixed).astype(jnp.bfloat16)
            advanced[:, c : c + HEAD] = total
            wide = total.astype(jnp.float32)
            squares = squares + wide * wide
        relay_out(h).start()
    row_sums = jnp.broadcast_to(jnp.sum(squares, axis=1, keepdims=True), (rows, HEAD))
    square_out[...] = row_sums.T[0:8, :]

    def sums_out(t):
        return pltpu.make_async_remote_copy(
            src_ref=square_out,
            dst_ref=square_in.at[t],
            send_sem=square_send_sem.at[t],
            recv_sem=square_recv_sem.at[t],
            device_id={"pipe": following, "tp": (tp + t) % n_tp},
            device_id_type=MESH,
        )

    for t in range(n_tp):
        sums_out(n_tp - 1 - t).start()

    for h in range(kv_heads):
        across(h).wait_send()
        pass_first(h).wait_send()
        pass_second(h).wait_send()

        @pl.when(z < NZ - 1)
        def _():
            up(h).wait_send()

    def drain(t, carry):
        slot, k, onward, first_of_beyond = place(t)
        for h in range(kv_heads):

            @pl.when(onward)
            def _():
                forward_z(slot, k, h).wait_send()

            @pl.when(jnp.logical_not(first_of_beyond))
            def _():
                forward_x(slot, h).wait_send()

        return carry

    lax.fori_loop(1, NZ + 1, drain, 0)

    for t in range(n_tp):
        sums_out(t).wait_recv()
    total = square_in[0, 0:1, :]
    for t in range(1, n_tp):
        total = total + square_in[t, 0:1, :]
    inverse = lax.rsqrt(total / (QUERY_HEADS * HEAD) + 1e-05)
    inverse = jnp.broadcast_to(inverse, (rows, rows)).T
    for h in range(kv_heads):
        relay_out(h).wait_recv()
        for g in range(group):
            c = (h * group + g) * HEAD
            wide = arrived_ref[:, c : c + HEAD].astype(jnp.float32)
            gain = gain_ref[c : c + HEAD].astype(jnp.float32)[None, :]
            normed_ref[:, c : c + HEAD] = (wide * inverse * gain).astype(jnp.bfloat16)
    for h in range(kv_heads):
        relay_out(h).wait_send()
    for t in range(n_tp):
        sums_out(t).wait_send()


def per_device(stream, queries, keys, values, segments, norm_gain):
    stream, queries, keys, values = stream[0], queries[0], keys[0], values[0]
    rows = queries.shape[0]
    kv_heads = keys.shape[1] // HEAD
    group = queries.shape[1] // keys.shape[1]
    block_rows = OH_ROWS + 2 * HEAD * kv_heads
    n_tp = lax.axis_size("tp")
    vmem = pl.BlockSpec(memory_space=pltpu.VMEM)
    anywhere = pl.BlockSpec(memory_space=pltpu.HBM)
    like_stream = jax.ShapeDtypeStruct(stream.shape, jnp.bfloat16)
    arrived, normed = pl.pallas_call(
        functools.partial(attention_kernel, kv_heads, group),
        out_shape=(like_stream, like_stream),
        in_specs=[anywhere] * 6,
        out_specs=(vmem, vmem),
        scratch_shapes=[
            pltpu.VMEM(queries.shape, jnp.bfloat16),
            pltpu.VMEM(keys.shape, jnp.bfloat16),
            pltpu.VMEM(values.shape, jnp.bfloat16),
            pltpu.VMEM(stream.shape, jnp.bfloat16),
            pltpu.VMEM(segments.shape, segments.dtype),
            pltpu.VMEM(norm_gain.shape, jnp.bfloat16),
            pltpu.VMEM(stream.shape, jnp.bfloat16),
            pltpu.VMEM((8, rows), jnp.float32),
            pltpu.VMEM((n_tp, 8, rows), jnp.float32),
            pltpu.VMEM((kv_heads, group * rows, 2 * HEAD), jnp.bfloat16),
            pltpu.VMEM((block_rows, rows), jnp.bfloat16),
            pltpu.VMEM((block_rows, rows), jnp.bfloat16),
            pltpu.VMEM((NZ, 2, block_rows, rows), jnp.bfloat16),
            pltpu.VMEM((kv_heads, group * rows, HEAD), jnp.float32),
            pltpu.VMEM((kv_heads, group * rows, 2 * HEAD), jnp.float32),
            pltpu.SemaphoreType.DMA((NZ, 2, kv_heads)),
            pltpu.SemaphoreType.DMA((NZ + 1, kv_heads)),
            pltpu.SemaphoreType.DMA((NZ + 1, kv_heads)),
            pltpu.SemaphoreType.DMA((kv_heads,)),
            pltpu.SemaphoreType.DMA((2, kv_heads)),
            pltpu.SemaphoreType.DMA((6,)),
            pltpu.SemaphoreType.DMA((kv_heads,)),
            pltpu.SemaphoreType.DMA((kv_heads,)),
            pltpu.SemaphoreType.DMA((n_tp,)),
            pltpu.SemaphoreType.DMA((n_tp,)),
        ],
        compiler_params=pltpu.CompilerParams(
            collective_id=0, has_side_effects=True, vmem_limit_bytes=63 * 1024 * 1024
        ),
    )(queries, keys, values, stream, segments, norm_gain)
    return (arrived[None], normed[None])


def solution(mesh):
    in_specs = (
        P("pipe", "ctx", "tp"),
        P("pipe", "ctx", "tp"),
        P("pipe", "ctx", "tp"),
        P("pipe", "ctx", "tp"),
        P("pipe", "ctx"),
        P("tp"),
    )
    out_specs = (P("pipe", "ctx", "tp"), P("pipe", "ctx", "tp"))
    return jax.shard_map(
        per_device, mesh=mesh, in_specs=in_specs, out_specs=out_specs, check_vma=False
    )
```

time: 94.9 us -> 88.2 us (0.929)
  local copies, waits for them, and re-layouts: 6.81 us -> 2.74 us
  Pallas kernels: 85.8 us -> 83.3 us
    unnamed x14 -> x4, local copies, waits for them, and re-layouts: 6.8 us -> 2.74 us
    pallas_call x1, Pallas kernels: 85.8 us -> 83.3 us  [per_device(): pl.pallas_call(functools.partial(attention_kernel, kv_heads, group), out_...]
where the time goes in v3:
time: 88.2 us; the launch traced here: 86.7 us
  Pallas kernels  83.3 us (94%)
  local copies, waits for them, and re-layouts  2.74 us (3%)
    pallas_call x1, Pallas kernels, per_device(): pl.pallas_call(functools.partial(attention_kernel, kv_heads, group), out_...  83.3 us
    unnamed x4, local copies, waits for them, and re-layouts  2.74 us

profile of v3, /device:TPU:24, one launch (start us, length us, event | category | flops | bytes accessed | tf_op | source)
XLA Modules:
  0.0 86.7 jit_solution(9132919404365244517)
XLA Ops:
  0.6 83.3 %shard_map.77 = (bf16[128,2048]{1,0:T(8,128)(2,1)}, bf16[128,2048]{1,0:T(8,128)(2,1)}) custom-call(bf16[128,2048]{1,0:T(8,128)(2,1)} %bitcast.6, bf16[128,512]{1,0:T(8,128)(2,1)} %bitcast.10, bf16[128,512]{1,0:T(8,128)(2,1)} %bitcast.11, bf16[128,2048]{1,0:T(8,128)(2,1)} %bitcast.7, s32[1,128]{1,0:T(1,128)} %seg_hbm.1, bf16[2048]{0:T(1024)(128)(2,1)} %gain_hbm.1), custom_call_target="tpu_custom_call" | custom-call | tf_op jit(solution)/shard_map/pallas_call | solution.py:374
  84.0 0.0 copy-start
  84.0 1.9 %copy.10 = bf16[1,128,2048]{2,1,0:T(8,128)(2,1)} copy(bf16[1,128,2048]{2,1,0:T(8,128)(2,1)} %bitcast.9) | data formatting | bytes 1048576
  85.9 0.0 copy-done
  85.9 0.8 copy.11
Async XLA Ops:
  84.0 2.0 %copy-start = (bf16[128,2048]{1,0:T(8,128)(2,1)S(1)}, bf16[128,2048]{1,0:T(8,128)(2,1)}, u32[]{:S(2)}) copy-start(bf16[128,2048]{1,0:T(8,128)(2,1)} %get-tuple-element.5) | copy-start | bytes 1572868

commit v4 on v3

--- a/solution.py
+++ b/solution.py
@@ -12,6 +12,7 @@
 MESH = pl.DeviceIdType.MESH
 NZ = 8
 OH_ROWS = 16
+LAG = 3
 FAR = float(2**20)
 LOG2E = 1.4426950408889634
 
@@ -200,7 +201,7 @@
         paired = jnp.where(t <= 2 * both, 1, 0)
         r = paired * ((t + 1) // 2) + (1 - paired) * (t - both)
         tall = jnp.where(z > NZ - z, 0, 1)
-        k = paired * ((t + 1) % 2) + (1 - paired) * tall
+        k = paired * (t % 2) + (1 - paired) * tall
         slot = (1 - k) * (z - r) + k * (z + r - 1)
         onward = (1 - k) * (NZ - 1 - z) + k * z > 0
         first_of_beyond = r + NZ * (1 - k) == 1
@@ -263,13 +264,20 @@
         attend_own(h)
 
     def step(t, carry):
-        now, before = place(t), place(t - 1)
+        now, before = place(t), place(t - LAG)
         for h in range(kv_heads):
             relay(now, h)
             attend(before, h)
         return carry
 
-    lax.fori_loop(2, NZ + 1, step, 0)
+    def step_without(t, carry):
+        now = place(t)
+        for h in range(kv_heads):
+            relay(now, h)
+        return carry
+
+    lax.fori_loop(2, LAG + 1, step_without, 0)
+    lax.fori_loop(LAG + 1, NZ + 1, step, 0)
 
     loads[4].wait()
     loads[5].wait()
@@ -286,10 +294,14 @@
             device_id_type=MESH,
         )
 
-    last = place(NZ)
     squares = jnp.zeros((rows, HEAD), jnp.float32)
     for h in range(kv_heads):
-        attend(last, h)
+
+        def rest(t, carry):
+            attend(place(t), h)
+            return carry
+
+        lax.fori_loop(NZ - LAG + 1, NZ + 1, rest, 0)
         for g in range(group):
             c = (h * group + g) * HEAD
             top_rows = slice(g * rows, (g + 1) * rows)

time: 88.2 us -> 79.5 us (0.901)
  the two profiles are of different devices: /device:TPU:24 before, /device:TPU:1 now
where the time goes in v4:
time: 79.5 us; the launch traced here: 79.3 us
  Pallas kernels  75.9 us (95%)
  local copies, waits for them, and re-layouts  2.74 us (3%)
    pallas_call x1, Pallas kernels, per_device(): pl.pallas_call(functools.partial(attention_kernel, kv_heads, group), out_...  75.9 us
    unnamed x4, local copies, waits for them, and re-layouts  2.74 us

profile of v4, /device:TPU:1, one launch (start us, length us, event | category | flops | bytes accessed | tf_op | source)
XLA Modules:
  0.0 79.3 jit_solution(6442983784496151913)
XLA Ops:
  0.6 75.9 %shard_map.77 = (bf16[128,2048]{1,0:T(8,128)(2,1)}, bf16[128,2048]{1,0:T(8,128)(2,1)}) custom-call(bf16[128,2048]{1,0:T(8,128)(2,1)} %bitcast.6, bf16[128,512]{1,0:T(8,128)(2,1)} %bitcast.10, bf16[128,512]{1,0:T(8,128)(2,1)} %bitcast.11, bf16[128,2048]{1,0:T(8,128)(2,1)} %bitcast.7, s32[1,128]{1,0:T(1,128)} %seg_hbm.1, bf16[2048]{0:T(1024)(128)(2,1)} %gain_hbm.1), custom_call_target="tpu_custom_call" | custom-call | tf_op jit(solution)/shard_map/pallas_call | solution.py:386
  76.6 0.0 copy-start
  76.6 1.9 %copy.10 = bf16[1,128,2048]{2,1,0:T(8,128)(2,1)} copy(bf16[1,128,2048]{2,1,0:T(8,128)(2,1)} %bitcast.9) | data formatting | bytes 1048576
  78.5 0.0 copy-done
  78.5 0.8 %copy.11 = bf16[1,128,2048]{2,1,0:T(8,128)(2,1)} copy(bf16[1,128,2048]{2,1,0:T(8,128)(2,1)S(1)} %bitcast.8) | data formatting | bytes 1048576
Async XLA Ops:
  76.6 2.0 %copy-start = (bf16[128,2048]{1,0:T(8,128)(2,1)S(1)}, bf16[128,2048]{1,0:T(8,128)(2,1)}, u32[]{:S(2)}) copy-start(bf16[128,2048]{1,0:T(8,128)(2,1)} %get-tuple-element.5) | copy-start | bytes 1572868

commit v5 on v4

--- a/solution.py
+++ b/solution.py
@@ -12,6 +12,7 @@
 MESH = pl.DeviceIdType.MESH
 NZ = 8
 OH_ROWS = 16
+NORM_COLUMNS = 1024
 LAG = 3
 FAR = float(2**20)
 LOG2E = 1.4426950408889634
@@ -25,15 +26,13 @@
     v_hbm,
     stream_hbm,
     seg_hbm,
-    gain_hbm,
     arrived_ref,
-    normed_ref,
+    inverse_ref,
     q_ref,
     k_ref,
     v_ref,
     stream_ref,
     seg_ref,
-    gain_ref,
     advanced,
     square_out,
     square_in,
@@ -77,7 +76,6 @@
                 (v_hbm, v_ref),
                 (q_hbm, q_ref),
                 (stream_hbm, stream_ref),
-                (gain_hbm, gain_ref),
             )
         )
     ]
@@ -156,18 +154,6 @@
             up(h).start()
 
         pass_first(h).start()
-
-    loads[3].wait()
-    seg_col = jnp.broadcast_to(seg_f, (rows, rows)).T
-    lane = lax.broadcasted_iota(jnp.int32, (rows, HEAD), 1)
-    penalty = jnp.where(
-        (lane < OH_ROWS) & (lane.astype(jnp.float32) != seg_col), -FAR, 0.0
-    ).astype(jnp.bfloat16)
-    for h in range(kv_heads):
-        for g in range(group):
-            c = (h * group + g) * HEAD
-            qa[h, g * rows : (g + 1) * rows, 0:HEAD] = q_ref[:, c : c + HEAD]
-            qa[h, g * rows : (g + 1) * rows, HEAD : 2 * HEAD] = penalty
 
     scale = LOG2E * HEAD ** (-0.5)
     height = group * rows
@@ -261,7 +247,18 @@
         pass_first(h).wait_recv()
         pass_second(h).start()
         relay(first, h)
-        attend_own(h)
+
+    loads[3].wait()
+    seg_col = jnp.broadcast_to(seg_f, (rows, rows)).T
+    lane = lax.broadcasted_iota(jnp.int32, (rows, HEAD), 1)
+    penalty = jnp.where(
+        (lane < OH_ROWS) & (lane.astype(jnp.float32) != seg_col), -FAR, 0.0
+    ).astype(jnp.bfloat16)
+    for h in range(kv_heads):
+        for g in range(group):
+            c = (h * group + g) * HEAD
+            qa[h, g * rows : (g + 1) * rows, 0:HEAD] = q_ref[:, c : c + HEAD]
+            qa[h, g * rows : (g + 1) * rows, HEAD : 2 * HEAD] = penalty
 
     def step(t, carry):
         now, before = place(t), place(t - LAG)
@@ -276,11 +273,18 @@
             relay(now, h)
         return carry
 
-    lax.fori_loop(2, LAG + 1, step_without, 0)
+    def step_own(t, carry):
+        now = place(t)
+        for h in range(kv_heads):
+            relay(now, h)
+            attend_own(h)
+        return carry
+
+    lax.fori_loop(2, LAG, step_without, 0)
+    lax.fori_loop(LAG, LAG + 1, step_own, 0)
     lax.fori_loop(LAG + 1, NZ + 1, step, 0)
 
     loads[4].wait()
-    loads[5].wait()
     width = group * HEAD
 
     def relay_out(h):
@@ -359,18 +363,24 @@
     for t in range(1, n_tp):
         total = total + square_in[t, 0:1, :]
     inverse = lax.rsqrt(total / (QUERY_HEADS * HEAD) + 1e-05)
-    inverse = jnp.broadcast_to(inverse, (rows, rows)).T
+    inverse_ref[...] = jnp.broadcast_to(inverse, (rows, rows)).T
     for h in range(kv_heads):
         relay_out(h).wait_recv()
-        for g in range(group):
-            c = (h * group + g) * HEAD
-            wide = arrived_ref[:, c : c + HEAD].astype(jnp.float32)
-            gain = gain_ref[c : c + HEAD].astype(jnp.float32)[None, :]
-            normed_ref[:, c : c + HEAD] = (wide * inverse * gain).astype(jnp.bfloat16)
     for h in range(kv_heads):
         relay_out(h).wait_send()
     for t in range(n_tp):
         sums_out(t).wait_send()
+
+
+def norm_kernel(in_ref, inverse_ref, gain_ref, arrived_ref, normed_ref):
+    inverse = inverse_ref[...]
+    for c in range(0, in_ref.shape[1], HEAD):
+        block = in_ref[:, c : c + HEAD]
+        arrived_ref[:, c : c + HEAD] = block
+        gain = gain_ref[c : c + HEAD].astype(jnp.float32)[None, :]
+        normed_ref[:, c : c + HEAD] = (block.astype(jnp.float32) * inverse * gain).astype(
+            jnp.bfloat16
+        )
 
 
 def per_device(stream, queries, keys, values, segments, norm_gain):
@@ -383,10 +393,10 @@
     vmem = pl.BlockSpec(memory_space=pltpu.VMEM)
     anywhere = pl.BlockSpec(memory_space=pltpu.HBM)
     like_stream = jax.ShapeDtypeStruct(stream.shape, jnp.bfloat16)
-    arrived, normed = pl.pallas_call(
+    arrived, inverse = pl.pallas_call(
         functools.partial(attention_kernel, kv_heads, group),
-        out_shape=(like_stream, like_stream),
-        in_specs=[anywhere] * 6,
+        out_shape=(like_stream, jax.ShapeDtypeStruct((rows, HEAD), jnp.float32)),
+        in_specs=[anywhere] * 5,
         out_specs=(vmem, vmem),
         scratch_shapes=[
             pltpu.VMEM(queries.shape, jnp.bfloat16),
@@ -394,7 +404,6 @@
             pltpu.VMEM(values.shape, jnp.bfloat16),
             pltpu.VMEM(stream.shape, jnp.bfloat16),
             pltpu.VMEM(segments.shape, segments.dtype),
-            pltpu.VMEM(norm_gain.shape, jnp.bfloat16),
             pltpu.VMEM(stream.shape, jnp.bfloat16),
             pltpu.VMEM((8, rows), jnp.float32),
             pltpu.VMEM((n_tp, 8, rows), jnp.float32),
@@ -409,7 +418,7 @@
             pltpu.SemaphoreType.DMA((NZ + 1, kv_heads)),
             pltpu.SemaphoreType.DMA((kv_heads,)),
             pltpu.SemaphoreType.DMA((2, kv_heads)),
-            pltpu.SemaphoreType.DMA((6,)),
+            pltpu.SemaphoreType.DMA((5,)),
             pltpu.SemaphoreType.DMA((kv_heads,)),
             pltpu.SemaphoreType.DMA((kv_heads,)),
             pltpu.SemaphoreType.DMA((n_tp,)),
@@ -418,7 +427,20 @@
         compiler_params=pltpu.CompilerParams(
             collective_id=0, has_side_effects=True, vmem_limit_bytes=63 * 1024 * 1024
         ),
-    )(queries, keys, values, stream, segments, norm_gain)
+    )(queries, keys, values, stream, segments)
+    columns = NORM_COLUMNS
+    tile = pl.BlockSpec((rows, columns), lambda i: (0, i))
+    arrived, normed = pl.pallas_call(
+        norm_kernel,
+        grid=(stream.shape[1] // columns,),
+        out_shape=(like_stream, like_stream),
+        in_specs=[
+            tile,
+            pl.BlockSpec((rows, HEAD), lambda i: (0, 0)),
+            pl.BlockSpec((columns,), lambda i: (i,)),
+        ],
+        out_specs=(tile, tile),
+    )(arrived, inverse, norm_gain)
     return (arrived[None], normed[None])
 
 

time: 79.5 us -> 78 us (0.981)
  the two profiles are of different devices: /device:TPU:1 before, /device:TPU:24 now
where the time goes in v5:
time: 78 us; the launch traced here: 76.7 us
  Pallas kernels  76.1 us (98%)
    pallas_call x1, Pallas kernels, per_device(): pl.pallas_call(functools.partial(attention_kernel, kv_heads, group), out_...  74 us
    pallas_call x1, Pallas kernels, per_device(): pl.pallas_call(norm_kernel, grid=(stream.shape[1] // columns,), out_shape...  2.07 us

profile of v5, /device:TPU:24, one launch (start us, length us, event | category | flops | bytes accessed | tf_op | source)
XLA Modules:
  0.0 76.7 jit_solution(18438073224129515935)
XLA Ops:
  0.6 74.0 %shard_map.77 = (bf16[128,2048]{1,0:T(8,128)(2,1)}, f32[128,128]{1,0:T(8,128)}) custom-call(bf16[128,2048]{1,0:T(8,128)(2,1)} %bitcast.6, bf16[128,512]{1,0:T(8,128)(2,1)} %bitcast.8, bf16[128,512]{1,0:T(8,128)(2,1)} %bitcast.9, bf16[128,2048]{1,0:T(8,128)(2,1)} %bitcast.7, s32[1,128]{1,0:T(1,128)} %seg_hbm.1), custom_call_target="tpu_custom_call" | custom-call | tf_op jit(solution)/shard_map/pallas_call | solution.py:396
  74.6 2.1 %shard_map.78 = (bf16[128,2048]{1,0:T(8,128)(2,1)}, bf16[128,2048]{1,0:T(8,128)(2,1)}) custom-call(bf16[128,2048]{1,0:T(8,128)(2,1)} %get-tuple-element.6.in_ref, f32[128,128]{1,0:T(8,128)} %get-tuple-element.7.inverse_ref, bf16[2048]{0:T(1024)(128)(2,1)} %gain_ref.1), custom_call_target="tpu_custom_call" | custom-call | tf_op jit(solution)/shard_map/pallas_call | solution.py:433

commit v6 on v5

--- a/solution.py
+++ b/solution.py
@@ -315,7 +315,8 @@
             advanced[:, c : c + HEAD] = total
             wide = total.astype(jnp.float32)
             squares = squares + wide * wide
-        relay_out(h).start()
+        if h < kv_heads - 1:
+            relay_out(h).start()
     row_sums = jnp.broadcast_to(jnp.sum(squares, axis=1, keepdims=True), (rows, HEAD))
     square_out[...] = row_sums.T[0:8, :]
 
@@ -331,6 +332,7 @@
 
     for t in range(n_tp):
         sums_out(n_tp - 1 - t).start()
+    relay_out(kv_heads - 1).start()
 
     for h in range(kv_heads):
         across(h).wait_send()

time: 78 us -> 78 us (level)
  no operation moved by 1% of the time
where the time goes in v6:
time: 78 us; the launch traced here: 76.7 us
  Pallas kernels  76.1 us (98%)
    pallas_call x1, Pallas kernels, per_device(): pl.pallas_call(functools.partial(attention_kernel, kv_heads, group), out_...  74 us
    pallas_call x1, Pallas kernels, per_device(): pl.pallas_call(norm_kernel, grid=(stream.shape[1] // columns,), out_shape...  2.07 us

profile of v6, /device:TPU:24, one launch (start us, length us, event | category | flops | bytes accessed | tf_op | source)
XLA Modules:
  0.0 76.7 jit_solution(10396798682878643790)
XLA Ops:
  0.6 74.0 %shard_map.77 = (bf16[128,2048]{1,0:T(8,128)(2,1)}, f32[128,128]{1,0:T(8,128)}) custom-call(bf16[128,2048]{1,0:T(8,128)(2,1)} %bitcast.6, bf16[128,512]{1,0:T(8,128)(2,1)} %bitcast.8, bf16[128,512]{1,0:T(8,128)(2,1)} %bitcast.9, bf16[128,2048]{1,0:T(8,128)(2,1)} %bitcast.7, s32[1,128]{1,0:T(1,128)} %seg_hbm.1), custom_call_target="tpu_custom_call" | custom-call | tf_op jit(solution)/shard_map/pallas_call | solution.py:398
  74.6 2.1 %shard_map.78 = (bf16[128,2048]{1,0:T(8,128)(2,1)}, bf16[128,2048]{1,0:T(8,128)(2,1)}) custom-call(bf16[128,2048]{1,0:T(8,128)(2,1)} %get-tuple-element.6.in_ref, f32[128,128]{1,0:T(8,128)} %get-tuple-element.7.inverse_ref, bf16[2048]{0:T(1024)(128)(2,1)} %gain_ref.1), custom_call_target="tpu_custom_call" | custom-call | tf_op jit(solution)/shard_map/pallas_call | solution.py:435

commit v7 on v6

--- a/solution.py
+++ b/solution.py
@@ -298,6 +298,31 @@
             device_id_type=MESH,
         )
 
+    for h in range(kv_heads):
+        across(h).wait_send()
+        pass_first(h).wait_send()
+        pass_second(h).wait_send()
+
+        @pl.when(z < NZ - 1)
+        def _():
+            up(h).wait_send()
+
+    def drain(t, carry):
+        slot, k, onward, first_of_beyond = place(t)
+        for h in range(kv_heads):
+
+            @pl.when(onward)
+            def _():
+                forward_z(slot, k, h).wait_send()
+
+            @pl.when(jnp.logical_not(first_of_beyond))
+            def _():
+                forward_x(slot, h).wait_send()
+
+        return carry
+
+    lax.fori_loop(1, NZ - LAG, drain, 0)
+
     squares = jnp.zeros((rows, HEAD), jnp.float32)
     for h in range(kv_heads):
 
@@ -334,30 +359,7 @@
         sums_out(n_tp - 1 - t).start()
     relay_out(kv_heads - 1).start()
 
-    for h in range(kv_heads):
-        across(h).wait_send()
-        pass_first(h).wait_send()
-        pass_second(h).wait_send()
-
-        @pl.when(z < NZ - 1)
-        def _():
-            up(h).wait_send()
-
-    def drain(t, carry):
-        slot, k, onward, first_of_beyond = place(t)
-        for h in range(kv_heads):
-
-            @pl.when(onward)
-            def _():
-                forward_z(slot, k, h).wait_send()
-
-            @pl.when(jnp.logical_not(first_of_beyond))
-            def _():
-                forward_x(slot, h).wait_send()
-
-        return carry
-
-    lax.fori_loop(1, NZ + 1, drain, 0)
+    lax.fori_loop(NZ - LAG, NZ + 1, drain, 0)
 
     for t in range(n_tp):
         sums_out(t).wait_recv()

time: 78 us -> 78.1 us (level)
  no operation moved by 1% of the time
where the time goes in v7:
time: 78.1 us; the launch traced here: 76.9 us
  Pallas kernels  76.2 us (98%)
    pallas_call x1, Pallas kernels, per_device(): pl.pallas_call(functools.partial(attention_kernel, kv_heads, group), out_...  74.1 us
    pallas_call x1, Pallas kernels, per_device(): pl.pallas_call(norm_kernel, grid=(stream.shape[1] // columns,), out_shape...  2.07 us

profile of v7, /device:TPU:24, one launch (start us, length us, event | category | flops | bytes accessed | tf_op | source)
XLA Modules:
  0.0 76.9 jit_solution(7509913021970018303)
XLA Ops:
  0.6 74.1 %shard_map.77 = (bf16[128,2048]{1,0:T(8,128)(2,1)}, f32[128,128]{1,0:T(8,128)}) custom-call(bf16[128,2048]{1,0:T(8,128)(2,1)} %bitcast.6, bf16[128,512]{1,0:T(8,128)(2,1)} %bitcast.8, bf16[128,512]{1,0:T(8,128)(2,1)} %bitcast.9, bf16[128,2048]{1,0:T(8,128)(2,1)} %bitcast.7, s32[1,128]{1,0:T(1,128)} %seg_hbm.1), custom_call_target="tpu_custom_call" | custom-call | tf_op jit(solution)/shard_map/pallas_call | solution.py:400
  74.8 2.1 %shard_map.78 = (bf16[128,2048]{1,0:T(8,128)(2,1)}, bf16[128,2048]{1,0:T(8,128)(2,1)}) custom-call(bf16[128,2048]{1,0:T(8,128)(2,1)} %get-tuple-element.6.in_ref, f32[128,128]{1,0:T(8,128)} %get-tuple-element.7.inverse_ref, bf16[2048]{0:T(1024)(128)(2,1)} %gain_ref.1), custom_call_target="tpu_custom_call" | custom-call | tf_op jit(solution)/shard_map/pallas_call | solution.py:437
